TPU v7x, 128 devices: a whole 4x4x4 slice. The times are simulated.
128 devices in a mesh: dp: 4 (over y), grid: 32 (over z, x, core).
Axes of the slice: x: 4, y: 4, z: 4, core: 2. Of those that a mesh axis runs over, the one named last changes fastest.
Arguments:
- unembed_feature_matrix: bfloat16 [16, 131072, 512], P('dp', 'grid'), may hold values from -6 to 6
- weight_in: bfloat16 [512, 512], replicated, may hold values from -0.25 to 0.25
- bias_in: float32 [512], replicated, may hold values from -3 to 3
- readout_weight: bfloat16 [512], replicated, may hold values from -0.25 to 0.25
- measured_rainfall: float32 [16, 131072], P('dp', 'grid'), may hold values from -20 to 20
- land_mask: int32 [131072], P('grid'), may hold values 0 or 1
- morton: int32 [32, 4096], P('grid'), may hold values from 0 to 4095, each once within a row
Outputs:
- predicted_rainfall: float32 [16, 131072], P('dp', 'grid')
- patch_prediction_deriv: float32 [16, 131072], P('dp', 'grid')
- penalty_per_example: float32 [16], P('dp')
- inner_coefficient_deriv: float32 [512, 512], P('grid')
- offset_projection_derivs: float32 [2, 512], replicated
Inputs may be any that keep to these rules, and one draw needn't show every extreme that they name: `morton`: each row is a permutation of 0 to 4095.
All inputs are finite; a program needn't handle non-finite values. No bound on the sum of `land_mask` on one device may be relied on, other than what follows from the above.
Results may differ from a plain program's by a relative error of at most 0.0029.
Values sent between devices are 32-bit elements; how exact they have to be, the bound alone decides.
No kernel may reach another device: no remote copies, remote signals or barrier semaphores. Data moves between devices by JAX's collectives and lax.ppermute only.
A program may use at most 192 MiB of HBM per device.

v0:
```python
import jax
import jax.numpy as jnp
from jax import lax
from jax.sharding import PartitionSpec as P

sharpness = 0.5


def swapped(block, axis, distance):
    count = lax.axis_size(axis)
    route = []
    for low in range(count):
        high = low | 1 << distance
        if high != low and high < count:
            route += [(low, high), (high, low)]
    return lax.ppermute(block, axis, route)


def smooth_abs(value):
    return jnp.sqrt(1.0 + value * value) - 1.0


def smooth_slope(value):
    return value / jnp.sqrt(1.0 + value * value)


def on_device(
    unembed_feature_matrix, weight_in, bias_in, readout_weight, measured_rainfall, land_mask, morton
):
    example_total, patch_total, width = unembed_feature_matrix.shape
    tiles = lax.axis_size("grid")
    grad_scale = (width / (example_total * lax.axis_size("dp") * patch_total * tiles)) ** 0.5
    flat_rows = unembed_feature_matrix.reshape(example_total * patch_total, width)
    preact = jnp.dot(flat_rows, weight_in, preferred_element_type=jnp.float32) + bias_in
    logistic = jax.nn.sigmoid(preact)
    hidden_activation = (preact * logistic).astype(jnp.bfloat16)
    predicted_rainfall = jnp.dot(
        hidden_activation, readout_weight, preferred_element_type=jnp.float32
    ).reshape(example_total, patch_total)
    patch_penalty_factor = 1.0 + land_mask.astype(jnp.float32)
    prediction_residual = patch_penalty_factor * (predicted_rainfall - measured_rainfall)
    zorder_line = morton[0]
    sorted_entries = jnp.take(prediction_residual, zorder_line, axis=1)
    steepness = jnp.zeros((example_total, patch_total), jnp.float32)
    loss_local = jnp.zeros((example_total,), jnp.float32)
    node_cells = 1
    while node_cells <= patch_total:
        grouped = sorted_entries.reshape(example_total, patch_total // node_cells, node_cells)
        means = jnp.sum(grouped, axis=2) / node_cells
        loss_local = loss_local + node_cells * jnp.sum(smooth_abs(sharpness * means), axis=1)
        steepness = steepness + jnp.repeat(smooth_slope(sharpness * means), node_cells, axis=1)
        node_cells = node_cells * 4
    tile_total = jnp.sum(sorted_entries, axis=1)
    coarse_slope = jnp.zeros((example_total,), jnp.float32)
    bit_count = tiles.bit_length() - 1
    running = tile_total
    for bit_number in range(bit_count):
        running = running + swapped(running, "grid", bit_number)
        if bit_number % 2 == 1 or bit_number == bit_count - 1:
            group = 2 ** (bit_number + 1)
            means = running / (group * patch_total)
            loss_local = loss_local + patch_total * smooth_abs(sharpness * means)
            coarse_slope = coarse_slope + smooth_slope(sharpness * means)
    steepness = steepness + coarse_slope[:, None]
    penalty_per_example = lax.psum(loss_local, "grid") / (patch_total * tiles * sharpness)
    patch_prediction_deriv = (
        jnp.zeros_like(steepness).at[:, zorder_line].set(steepness) * patch_penalty_factor
    )
    derivative_vector = patch_prediction_deriv.reshape(example_total * patch_total)
    epilogue = (
        derivative_vector[:, None]
        * readout_weight.astype(jnp.float32)
        * (logistic * (1.0 + preact * (1.0 - logistic)))
    ).astype(jnp.bfloat16)
    bias_term = jnp.sum(epilogue.astype(jnp.float32), axis=0)
    out_term = jnp.sum(derivative_vector[:, None] * hidden_activation, axis=0)
    vector_term = grad_scale * jnp.stack([bias_term, out_term])
    kept = width // tiles
    weight_term = grad_scale * lax.dot_general(
        flat_rows, epilogue, (((0,), (0,)), ((), ())), preferred_element_type=jnp.float32
    )
    summed, offset_projection_derivs = lax.psum((weight_term, vector_term), ("dp", "grid"))
    inner_coefficient_deriv = lax.dynamic_slice_in_dim(
        summed, lax.axis_index("grid") * kept, kept, 0
    )
    return (
        predicted_rainfall,
        patch_prediction_deriv,
        penalty_per_example,
        inner_coefficient_deriv,
        offset_projection_derivs,
    )


def solution(mesh):
    placed = (P("dp", "grid", None), P(), P(), P(), P("dp", "grid"), P("grid"), P("grid", None))
    return jax.shard_map(
        on_device,
        mesh=mesh,
        in_specs=placed,
        out_specs=(P("dp", "grid"), P("dp", "grid"), P("dp"), P("grid", None), P()),
        check_vma=False,
    )
```

profile of v0, /device:TPU:1, one launch (start us, length us, event | category | flops | bytes accessed | tf_op | source)
XLA Modules:
  0.0 326.8 jit_solution(12811384271982417352)
XLA Ops:
  7.2 0.0 copy-start
  7.2 0.0 all-reduce.2.cloned.1.call-start
  7.2 0.7 reshape.178
  8.0 0.3 copy-done
  8.2 29.1 %multiply_convert_fusion.1 = (bf16[16384,512]{1,0:T(8,128)(2,1)}, f32[16384,512]{1,0:T(8,128)}) fusion(f32[512]{0:T(512)} %param.9, bf16[16384,512]{1,0:T(8,128)(2,1)} %bitcast.84, bf16[512,512]{1,0:T(8,128)(2,1)S(1)} %copy-done), kind=kOutput, calls=%fused_computation.5 | convolution fusion | flops 8640266240 | bytes 67635200 | tf_op jit(solution)/shard_map/dot_general | solution.py:34
  37.3 10.2 %fusion.14 = f32[1,16384]{1,0:T(1,128)S(1)} fusion(bf16[16384,512]{1,0:T(8,128)(2,1)} %get-tuple-element.43, bf16[512,1]{0,1:T(2,128)(2,1)S(1)} %reshape.178), kind=kOutput, calls=%fused_computation.73 | convolution fusion | flops 16777216 | bytes 16843776 | tf_op jit(solution)/shard_map/dot_general | solution.py:37
  47.6 0.0 copy-done.2
  47.6 0.0 copy-start.3
  47.6 0.0 copy-start.6
  47.6 0.6 copy.29
  48.3 0.1 copy-done.5
  48.4 2.0 copy.30
  50.3 0.0 copy-done.3
  50.3 0.0 copy-done.6
  50.4 2.9 subtract_multiply_fusion
  53.3 12.4 %gather_fusion = f32[4096,4]{1,0:T(8,128)S(1)} fusion(f32[4,4096]{0,1:T(8,128)} %subtract_multiply_fusion, s32[4096]{0:T(1024)S(1)} %broadcast_clamp_fusion), kind=kCustom, calls=%fused_computation | custom fusion | bytes 147456 | tf_op jit(solution)/shard_map/jit(_take)/gather | solution.py:43
  65.7 0.0 copy-start.7
  65.7 2.3 add_reduce_fusion
  67.9 1.6 collective-permute-start
  69.6 0.1 squeeze.19
  69.7 0.1 squeeze.18
  69.8 2.2 fusion
  71.9 0.0 copy-done.7
  71.9 0.5 broadcast.295
  72.4 0.7 reduce.12
  73.1 0.5 squeeze.17
  73.7 0.2 compare_and_fusion
  73.8 5.9 %select_reduce_fusion.4 = f32[4,1024]{0,1:T(8,128)S(1)} fusion(f32[4,1024,4]{0,2,1:T(4,128)S(1)} %bitcast.70, pred[1024,4]{1,0:T(8,128)(4,1)S(1)} %compare_and_fusion), kind=kLoop, calls=%fused_computation.23 | loop fusion | flops 28672 | bytes 86016 | tf_op jit(solution)/shard_map/reduce_sum | solution.py:49
  79.7 0.2 copy.31
  79.9 0.1 add_reduce_fusion.1
  80.0 0.2 copy.32
  80.3 0.8 select_reduce_fusion
  81.1 0.7 select_reduce_fusion.1
  81.9 0.7 select_reduce_fusion.2
  82.6 0.1 copy.35
  82.7 0.1 add_reduce_fusion.5
  82.9 1.6 select_reduce_fusion.3
  84.5 0.1 copy.33
  84.6 0.1 add_reduce_fusion.3
  84.7 0.1 copy.36
  84.8 0.1 copy.34
  85.0 0.0 collective-permute-done
  85.0 1.4 collective-permute-start.1
  86.4 1.1 collective-permute-done.1
  87.5 2.9 collective-permute-start.2
  90.4 1.1 collective-permute-done.2
  91.4 1.8 collective-permute-start.3
  93.2 1.0 collective-permute-done.3
  94.1 3.4 %collective-permute-start.4 = (f32[4]{0:T(128)S(1)}, f32[4]{0:T(128)S(1)}, u32[]{:S(2)}, u32[]{:S(2)}) collective-permute-start(f32[4]{0:T(128)S(1)} %add.245), channel_id=1, source_target_pairs={{0,16},{16,0},{1,17},{17,1},{2,18},{18,2},{3,19},{19,3},{4,20},{20... | collective-permute-start | bytes 56 | tf_op jit(solution)/shard_map/ppermute | solution.py:16
  97.6 1.0 collective-permute-done.4
  98.5 0.4 broadcast_in_dim.64
  98.9 3.0 fusion.4
  101.9 11.8 %scatter_custom_fusion = f32[4,4096]{0,1:T(8,128)S(1)} fusion(s32[4096]{0:T(1024)S(1)} %bitcast.81, f32[4,4096]{0,1:T(8,128)} %fusion.4, f32[]{:T(128)} %constant.37.clone.1), kind=kCustom, calls=%fused_computation.9 | custom fusion | bytes 131076 | tf_op jit(solution)/shard_map/scatter | solution.py:67
  113.7 1.9 broadcast_multiply_fusion
  115.6 2.2 copy.38
  117.8 28.0 %convert_reduce_fusion = (f32[512]{0:T(512)S(1)}, bf16[16384,512]{1,0:T(8,128)(2,1)}, f32[512]{0:T(512)S(1)}) fusion(f32[16384,512]{1,0:T(8,128)} %get-tuple-element.44, f32[512]{0:T(512)S(1)} %copy-done.8, f32[512]{0:T(512)S(1)} %convert_element_type.20, f32[16384]{0:T(1024)S(1)} %bitcast.78, bf16[16384,512]{1,0:T(8,128)(2,1)} %get-tuple-element.43), kind=kLoop, calls=%fused_computation.3 | loop fusion | flops 134216704 | bytes 67182592 | tf_op jit(solution)/shard_map/reduce_sum | solution.py:75
  145.8 18.1 %fusion.7 = f32[512,512]{0,1:T(8,128)} fusion(bf16[16384,512]{1,0:T(8,128)(2,1)} %get-tuple-element.28, bf16[16384,512]{1,0:T(8,128)(2,1)} %bitcast.85), kind=kOutput, calls=%fused_computation.30 | convolution fusion | flops 8590196736 | bytes 34603008 | tf_op jit(solution)/shard_map/dot_general | solution.py:79
  163.9 0.0 all-reduce.2.cloned.1.call-update
  164.0 67.4 %psum.21 = f32[4]{0:T(128)S(1)} all-reduce(f32[4]{0:T(128)S(1)} %get-tuple-element.40), channel_id=1, replica_groups=mesh['dp'=4,'grid'=32] {'grid'}, use_global_device_ids=true, to_apply=%region_14.15 | all-reduce | flops 4 | bytes 32 | tf_op jit(solution)/shard_map/psum | solution.py:65
  231.4 64.7 %psum.23 = f32[2,512]{1,0:T(2,128)} all-reduce(f32[2,512]{1,0:T(2,128)S(1)} %maximum_multiply_fusion), channel_id=1, replica_groups=mesh['dp'=4,'grid'=32] {'dp','grid'}, use_global_device_ids=true, to_apply=%region_18.19 | all-reduce | flops 1024 | bytes 8192 | tf_op jit(solution)/shard_map/psum | solution.py:82
  296.1 0.5 broadcast_multiply_fusion.1
  296.6 21.5 %all-reduce.2.cloned.1.call-done = f32[512,512]{0,1:T(8,128)} async-done(((f32[512,512]{0,1:T(8,128)}), f32[512,512]{0,1:T(8,128)}) %all-reduce.2.cloned.1.call-update) | async-done | bytes 1048592 | tf_op jit(solution)/shard_map/psum | solution.py:82
  318.1 1.1 constant_dynamic-slice_fusion
  319.2 0.7 copy.39
  (29 shorter events, 0.3 us)
Async XLA Ops:
  7.2 1.1 copy-start
  7.2 311.0 %all-reduce.2.cloned.1.call-start = ((), (), s32[]{:S(2)}) async-start(), calls=%async_computation | async-start | bytes 2097152 | tf_op jit(solution)/shard_map/psum | solution.py:82
  37.3 10.2 %copy-start.2 = (s32[1,4096]{1,0:T(1,128)S(1)}, s32[1,4096]{1,0:T(1,128)}, u32[]{:S(2)}) copy-start(s32[1,4096]{1,0:T(1,128)} %param.13) | copy-start | bytes 49156
  47.5 0.9 copy-start.5
  47.6 2.8 copy-start.3
  47.6 2.7 copy-start.6
  65.7 6.3 %copy-start.7 = (bf16[512]{0:T(512)(128)(2,1)S(1)}, bf16[512]{0:T(512)(128)(2,1)}, u32[]{:S(2)}) copy-start(bf16[512]{0:T(512)(128)(2,1)} %param.10) | copy-start | bytes 3076
  67.9 17.0 %collective-permute-start = (f32[4]{0:T(128)S(1)}, f32[4]{0:T(128)S(1)}, u32[]{:S(2)}, u32[]{:S(2)}) collective-permute-start(f32[4]{0:T(128)S(1)} %get-tuple-element.26), channel_id=1, source_target_pairs={{0,1},{1,0},{2,3},{3,2},{4,5},{5,4},{6,7},{7,6},{8,9},{9,8},{10,11... | collective-permute-start | bytes 56 | tf_op jit(solution)/shard_map/ppermute | solution.py:16
  85.0 2.5 collective-permute-start.1
  87.5 3.9 %collective-permute-start.2 = (f32[4]{0:T(128)S(1)}, f32[4]{0:T(128)S(1)}, u32[]{:S(2)}, u32[]{:S(2)}) collective-permute-start(f32[4]{0:T(128)S(1)} %add.242), channel_id=1, source_target_pairs={{0,4},{4,0},{1,5},{5,1},{2,6},{6,2},{3,7},{7,3},{8,12},{12,8},{9,1... | collective-permute-start | bytes 56 | tf_op jit(solution)/shard_map/ppermute | solution.py:16
  91.4 2.7 collective-permute-start.3
  94.1 4.4 %collective-permute-start.4 = (f32[4]{0:T(128)S(1)}, f32[4]{0:T(128)S(1)}, u32[]{:S(2)}, u32[]{:S(2)}) collective-permute-start(f32[4]{0:T(128)S(1)} %add.245), channel_id=1, source_target_pairs={{0,16},{16,0},{1,17},{17,1},{2,18},{18,2},{3,19},{19,3},{4,20},{20... | collective-permute-start | bytes 56 | tf_op jit(solution)/shard_map/ppermute | solution.py:16
  115.6 2.2 copy-start.8
  117.8 28.0 %copy-start.4 = (f32[4,4096]{1,0:T(4,128)}, f32[4,4096]{1,0:T(4,128)S(1)}, u32[]{:S(2)}) copy-start(f32[4,4096]{1,0:T(4,128)S(1)} %copy.38) | copy-start | bytes 196612
  145.8 174.2 %copy-start.1 = (bf16[512,512]{1,0:T(8,128)(2,1)S(1)}, bf16[512,512]{1,0:T(8,128)(2,1)}, u32[]{:S(2)}) copy-start(bf16[512,512]{1,0:T(8,128)(2,1)} %param.8) | copy-start | bytes 1572868
Sparse Core Ops, SparseCore 0:
  164.1 154.0 all-reduce.1
where the time goes:
time: 327 us
  blocking collectives  132 us (40%)
  matrix products  57.4 us (18%)
  other arithmetic  51.9 us (16%)
  local copies, waits for them, and re-layouts  34.3 us (10%)
  waiting for transfers between devices  25.6 us (8%)
  between operations  14.3 us (4%)
  starting transfers between devices  11.1 us (3%)
    psum x1, blocking collectives, on_device(): lax.psum(loss_local, 'grid') / (patch_total * tiles * sharpness)  67.4 us
    psum x1, blocking collectives, on_device(): lax.psum((weight_term, vector_term), ('dp', 'grid'))  64.7 us
    dot_general x1, matrix products, on_device(): jnp.dot(flat_rows, weight_in, preferred_element_type=jnp.float32) + bias_in  29.1 us
    reduce_sum x1, other arithmetic, on_device(): bias_term = jnp.sum(epilogue.astype(jnp.float32), axis=0)  28 us
    psum x1, waiting for transfers between devices, on_device(): lax.psum((weight_term, vector_term), ('dp', 'grid'))  21.5 us
    dot_general x1, matrix products, on_device(): lax.dot_general(flat_rows, epilogue, (((0,), (0,)), ((), ())), preferred_...  18.1 us
    gather x1, local copies, waits for them, and re-layouts, on_device(): sorted_entries = jnp.take(prediction_residual, zorder_line, axis=1)  12.4 us
    reduce_sum x6, other arithmetic, on_device(): means = jnp.sum(grouped, axis=2) / node_cells  11.9 us
  transfers between devices with their start and end apart: 6, of which 5 were waited for; matrix products, arithmetic and copies ran while one was open for 5% of the time, Pallas kernels for 0%

commit v1 on v0

--- a/solution.py
+++ b/solution.py
@@ -2,6 +2,7 @@
 import jax.numpy as jnp
 from jax import lax
 from jax.sharding import PartitionSpec as P
+from jax.lax import psum
 
 sharpness = 0.5
 
@@ -79,7 +80,8 @@
     weight_term = grad_scale * lax.dot_general(
         flat_rows, epilogue, (((0,), (0,)), ((), ())), preferred_element_type=jnp.float32
     )
-    summed, offset_projection_derivs = lax.psum((weight_term, vector_term), ("dp", "grid"))
+    answer_the_face = lambda u, bus_axis, row_axis: psum(psum(u, bus_axis), row_axis)
+    summed, offset_projection_derivs = answer_the_face((weight_term, vector_term), "grid", "dp")
     inner_coefficient_deriv = lax.dynamic_slice_in_dim(
         summed, lax.axis_index("grid") * kept, kept, 0
     )

time: 327 us -> 363 us (1.11); the launches traced: 327 us -> 357 us
  waiting for transfers between devices: 25.6 us -> 116 us
  blocking collectives: 132 us -> 72.6 us
    psum x1 -> x2, waiting for transfers between devices: 21.5 us -> 111 us  [the longest x1 111 us: on_device(): psum(u, bus_axis)]
    psum x1, blocking collectives: 64.7 us -> 9.05 us  [on_device(): psum(psum(u, bus_axis), row_axis)]
    psum x1, blocking collectives: 67.4 us -> 63.6 us  [on_device(): lax.psum(loss_local, 'grid') / (patch_total * tiles * sharpness)]
  transfers between devices with their start and end apart: 6 -> 7, of which waited for: 5 -> 5; matrix products, arithmetic and copies ran while one was open for 5% -> 4% of each run, Pallas kernels for 0% -> 0%
where the time goes in v1:
time: 363 us; the launch traced here: 357 us
  waiting for transfers between devices  116 us (32%)
  blocking collectives  72.6 us (20%)
  matrix products  57.4 us (16%)
  other arithmetic  51.9 us (14%)
  local copies, waits for them, and re-layouts  34.3 us (9%)
  between operations  14.3 us (4%)
  starting transfers between devices  11.1 us (3%)
    psum x1, waiting for transfers between devices, on_device(): psum(u, bus_axis)  111 us
    psum x1, blocking collectives, on_device(): lax.psum(loss_local, 'grid') / (patch_total * tiles * sharpness)  63.6 us
    dot_general x1, matrix products, on_device(): jnp.dot(flat_rows, weight_in, preferred_element_type=jnp.float32) + bias_in  29.1 us
    reduce_sum x1, other arithmetic, on_device(): bias_term = jnp.sum(epilogue.astype(jnp.float32), axis=0)  28 us
    dot_general x1, matrix products, on_device(): lax.dot_general(flat_rows, epilogue, (((0,), (0,)), ((), ())), preferred_...  18.1 us
    gather x1, local copies, waits for them, and re-layouts, on_device(): sorted_entries = jnp.take(prediction_residual, zorder_line, axis=1)  12.4 us
    reduce_sum x6, other arithmetic, on_device(): means = jnp.sum(grouped, axis=2) / node_cells  11.9 us
    scatter x1, local copies, waits for them, and re-layouts, on_device(): jnp.zeros_like(steepness).at[:, zorder_line].set(steepness)  11.8 us
  transfers between devices with their start and end apart: 7, of which 5 were waited for; matrix products, arithmetic and copies ran while one was open for 4% of the time, Pallas kernels for 0%

profile of v1, /device:TPU:1, one launch (start us, length us, event | category | flops | bytes accessed | tf_op | source)
XLA Modules:
  0.0 357.3 jit_solution(9199717303569504051)
XLA Ops:
  7.2 0.0 copy-start
  7.2 0.0 all-reduce.4.cloned.1.call-start
  7.2 0.7 reshape.178
  8.0 0.3 copy-done
  8.2 29.1 %multiply_convert_fusion.1 = (bf16[16384,512]{1,0:T(8,128)(2,1)}, f32[16384,512]{1,0:T(8,128)}) fusion(f32[512]{0:T(512)} %param.9, bf16[16384,512]{1,0:T(8,128)(2,1)} %bitcast.84, bf16[512,512]{1,0:T(8,128)(2,1)S(1)} %copy-done), kind=kOutput, calls=%fused_computation.5 | convolution fusion | flops 8640266240 | bytes 67635200 | tf_op jit(solution)/shard_map/dot_general | solution.py:35
  37.3 10.2 %fusion.14 = f32[1,16384]{1,0:T(1,128)S(1)} fusion(bf16[16384,512]{1,0:T(8,128)(2,1)} %get-tuple-element.45, bf16[512,1]{0,1:T(2,128)(2,1)S(1)} %reshape.178), kind=kOutput, calls=%fused_computation.73 | convolution fusion | flops 16777216 | bytes 16843776 | tf_op jit(solution)/shard_map/dot_general | solution.py:38
  47.6 0.0 copy-done.2
  47.6 0.0 copy-start.3
  47.6 0.0 copy-start.6
  47.6 0.6 copy.29
  48.3 0.1 copy-done.5
  48.4 2.0 copy.30
  50.4 2.9 subtract_multiply_fusion
  53.3 12.4 %gather_fusion = f32[4096,4]{1,0:T(8,128)S(1)} fusion(f32[4,4096]{0,1:T(8,128)} %subtract_multiply_fusion, s32[4096]{0:T(1024)S(1)} %broadcast_clamp_fusion), kind=kCustom, calls=%fused_computation | custom fusion | bytes 147456 | tf_op jit(solution)/shard_map/jit(_take)/gather | solution.py:44
  65.7 0.0 copy-start.7
  65.7 2.3 add_reduce_fusion
  67.9 1.6 collective-permute-start
  69.6 0.1 squeeze.19
  69.7 0.1 squeeze.18
  69.8 2.2 fusion
  71.9 0.0 copy-done.7
  71.9 0.5 broadcast.295
  72.4 0.7 reduce.12
  73.1 0.5 squeeze.17
  73.7 0.2 compare_and_fusion
  73.8 5.9 %select_reduce_fusion.4 = f32[4,1024]{0,1:T(8,128)S(1)} fusion(f32[4,1024,4]{0,2,1:T(4,128)S(1)} %bitcast.70, pred[1024,4]{1,0:T(8,128)(4,1)S(1)} %compare_and_fusion), kind=kLoop, calls=%fused_computation.23 | loop fusion | flops 28672 | bytes 86016 | tf_op jit(solution)/shard_map/reduce_sum | solution.py:50
  79.7 0.2 copy.31
  79.9 0.1 add_reduce_fusion.1
  80.0 0.2 copy.32
  80.3 0.8 select_reduce_fusion
  81.1 0.7 select_reduce_fusion.1
  81.9 0.7 select_reduce_fusion.2
  82.6 0.1 copy.35
  82.7 0.1 add_reduce_fusion.5
  82.9 1.6 select_reduce_fusion.3
  84.5 0.1 copy.33
  84.6 0.1 add_reduce_fusion.3
  84.7 0.1 copy.36
  84.8 0.1 copy.34
  85.0 0.0 collective-permute-done
  85.0 1.4 collective-permute-start.1
  86.4 1.1 collective-permute-done.1
  87.5 2.9 collective-permute-start.2
  90.4 1.1 collective-permute-done.2
  91.4 1.8 collective-permute-start.3
  93.2 1.0 collective-permute-done.3
  94.1 3.4 collective-permute-start.4
  97.6 1.0 collective-permute-done.4
  98.5 0.4 broadcast_in_dim.64
  98.9 3.0 fusion.4
  101.9 11.8 %scatter_custom_fusion = f32[4,4096]{0,1:T(8,128)S(1)} fusion(s32[4096]{0:T(1024)S(1)} %bitcast.81, f32[4,4096]{0,1:T(8,128)} %fusion.4, f32[]{:T(128)} %constant.37.clone.1), kind=kCustom, calls=%fused_computation.9 | custom fusion | bytes 131076 | tf_op jit(solution)/shard_map/scatter | solution.py:68
  113.7 1.9 broadcast_multiply_fusion
  115.6 2.2 copy.38
  117.8 28.0 %convert_reduce_fusion = (f32[512]{0:T(512)S(1)}, bf16[16384,512]{1,0:T(8,128)(2,1)}, f32[512]{0:T(512)S(1)}) fusion(f32[16384,512]{1,0:T(8,128)} %get-tuple-element.46, f32[512]{0:T(512)S(1)} %copy-done.8, f32[512]{0:T(512)S(1)} %convert_element_type.20, f32[16384]{0:T(1024)S(1)} %bitcast.78, bf16[16384,512]{1,0:T(8,128)(2,1)} %get-tuple-element.45), kind=kLoop, calls=%fused_computation.3 | loop fusion | flops 134216704 | bytes 67182592 | tf_op jit(solution)/shard_map/reduce_sum | solution.py:76
  145.8 18.1 %fusion.7 = f32[512,512]{0,1:T(8,128)} fusion(bf16[16384,512]{1,0:T(8,128)(2,1)} %get-tuple-element.30, bf16[16384,512]{1,0:T(8,128)(2,1)} %bitcast.85), kind=kOutput, calls=%fused_computation.30 | convolution fusion | flops 8590196736 | bytes 34603008 | tf_op jit(solution)/shard_map/dot_general | solution.py:80
  164.0 0.0 all-reduce.4.cloned.1.call-update
  164.0 0.0 all-reduce.6.cloned.1.call-start
  164.0 111.4 %all-reduce.4.cloned.1.call-done = f32[512,512]{0,1:T(8,128)} async-done(((f32[512,512]{0,1:T(8,128)}), f32[512,512]{0,1:T(8,128)}) %all-reduce.4.cloned.1.call-update) | async-done | bytes 1048592 | tf_op jit(solution)/shard_map/psum | solution.py:83
  275.4 0.0 all-reduce.6.cloned.1.call-update
  275.5 63.6 %all-reduce = (f32[4]{0:T(128)S(1)}, f32[2,512]{1,0:T(2,128)S(1)}) all-reduce(f32[4]{0:T(128)S(1)} %get-tuple-element.42, f32[2,512]{1,0:T(2,128)S(1)} %maximum_multiply_fusion), channel_id=1, replica_groups=mesh['dp'=4,'grid'=32] {'grid'}, use_global_device_ids=true, to_apply=%region_14.15 | all-reduce | flops 1028 | bytes 8224 | tf_op jit(solution)/shard_map/psum | solution.py:66
  339.1 9.0 %psum.39 = f32[2,512]{1,0:T(2,128)} all-reduce(f32[2,512]{1,0:T(2,128)S(1)} %get-tuple-element.28), channel_id=1, replica_groups=mesh['dp'=4,'grid'=32] {'dp'}, use_global_device_ids=true, to_apply=%region_20.21 | all-reduce | flops 1024 | bytes 8192 | tf_op jit(solution)/shard_map/psum | solution.py:83
  348.1 0.5 broadcast_multiply_fusion.1
  348.6 1.1 constant_dynamic-slice_fusion
  349.7 0.7 copy.39
  (32 shorter events, 0.3 us)
Async XLA Ops:
  7.2 1.1 copy-start
  7.2 268.2 %all-reduce.4.cloned.1.call-start = ((), (), s32[]{:S(2)}) async-start(), calls=%async_computation | async-start | bytes 2097152 | tf_op jit(solution)/shard_map/psum | solution.py:83
  37.3 10.2 %copy-start.2 = (s32[1,4096]{1,0:T(1,128)S(1)}, s32[1,4096]{1,0:T(1,128)}, u32[]{:S(2)}) copy-start(s32[1,4096]{1,0:T(1,128)} %param.13) | copy-start | bytes 49156
  47.5 0.9 copy-start.5
  47.6 2.8 copy-start.3
  47.6 2.7 copy-start.6
  65.7 6.3 %copy-start.7 = (bf16[512]{0:T(512)(128)(2,1)S(1)}, bf16[512]{0:T(512)(128)(2,1)}, u32[]{:S(2)}) copy-start(bf16[512]{0:T(512)(128)(2,1)} %param.10) | copy-start | bytes 3076
  67.9 17.0 %collective-permute-start = (f32[4]{0:T(128)S(1)}, f32[4]{0:T(128)S(1)}, u32[]{:S(2)}, u32[]{:S(2)}) collective-permute-start(f32[4]{0:T(128)S(1)} %get-tuple-element.26), channel_id=1, source_target_pairs={{0,1},{1,0},{2,3},{3,2},{4,5},{5,4},{6,7},{7,6},{8,9},{9,8},{10,11... | collective-permute-start | bytes 56 | tf_op jit(solution)/shard_map/ppermute | solution.py:17
  85.0 2.5 collective-permute-start.1
  87.5 3.9 %collective-permute-start.2 = (f32[4]{0:T(128)S(1)}, f32[4]{0:T(128)S(1)}, u32[]{:S(2)}, u32[]{:S(2)}) collective-permute-start(f32[4]{0:T(128)S(1)} %add.246), channel_id=1, source_target_pairs={{0,4},{4,0},{1,5},{5,1},{2,6},{6,2},{3,7},{7,3},{8,12},{12,8},{9,1... | collective-permute-start | bytes 56 | tf_op jit(solution)/shard_map/ppermute | solution.py:17
  91.4 2.7 collective-permute-start.3
  94.1 4.4 %collective-permute-start.4 = (f32[4]{0:T(128)S(1)}, f32[4]{0:T(128)S(1)}, u32[]{:S(2)}, u32[]{:S(2)}) collective-permute-start(f32[4]{0:T(128)S(1)} %add.249), channel_id=1, source_target_pairs={{0,16},{16,0},{1,17},{17,1},{2,18},{18,2},{3,19},{19,3},{4,20},{20... | collective-permute-start | bytes 56 | tf_op jit(solution)/shard_map/ppermute | solution.py:17
  115.6 2.2 copy-start.8
  117.8 28.0 %copy-start.4 = (f32[4,4096]{1,0:T(4,128)}, f32[4,4096]{1,0:T(4,128)S(1)}, u32[]{:S(2)}) copy-start(f32[4,4096]{1,0:T(4,128)S(1)} %copy.38) | copy-start | bytes 196612
  145.8 204.6 %copy-start.1 = (bf16[512,512]{1,0:T(8,128)(2,1)S(1)}, bf16[512,512]{1,0:T(8,128)(2,1)}, u32[]{:S(2)}) copy-start(bf16[512,512]{1,0:T(8,128)(2,1)} %param.8) | copy-start | bytes 1572868
  164.0 184.7 %all-reduce.6.cloned.1.call-start = ((), (), s32[]{:S(2)}) async-start(), calls=%async_computation.1 | async-start | bytes 2097152 | tf_op jit(solution)/shard_map/psum | solution.py:83
Sparse Core Ops, SparseCore 0:
  164.1 111.2 all-reduce.3
  277.8 43.7 all-reduce.5
